TPU v7x, 32 devices: a whole 2x2x4 slice. The times are simulated.
32 devices in a mesh: section: 4 (over y, x), dp: 8 (over z, core).
Axes of the slice: x: 2, y: 2, z: 4, core: 2. Of those that a mesh axis runs over, the one named last changes fastest.
Arguments:
- hidden: bfloat16 [512, 4096], P('dp'), may hold values from -6 to 6
- neighbours: bfloat16 [8, 128, 4096], P('dp'), may hold values from -28 to 28
- norm_gain: float32 [4, 4096], P('section'), may hold values from 0.5 to 2
- w_query: bfloat16 [4, 4096, 4096], P('section', None, 'dp'), may hold values from -0.09375 to 0.09375
- w_kv: bfloat16 [4, 4096, 2, 4096], P('section', None, None, 'dp'), may hold values from -0.09375 to 0.09375
- w_out: bfloat16 [4, 4096, 4096], P('section', 'dp'), may hold values from -0.375 to 0.375
Outputs:
- section_outputs: bfloat16 [4, 512, 4096], P('section', 'dp')
All inputs are finite; a program needn't handle non-finite values.
Results may differ from a plain program's by a relative error of at most 0.03.
The roundings to bfloat16 on the way count: a program that leaves them out, or rounds other values in their place, can miss the bound.
Values may be sent and summed in bfloat16 or wider, within the bound.
A program may use at most 128 MiB of HBM per device.

v0:
```python
import jax
import jax.numpy as jnp
from jax import lax
from jax.sharding import PartitionSpec as P

DH = 128
BLOCK_LEN = 64
MB = 8


def passed_along(block, axis, distance):
    devices = range(lax.axis_size(axis))
    route = [(i - distance, i) for i in devices if i - distance in devices]
    return lax.ppermute(block, axis, route)


def per_device(hidden, neighbours, norm_gain, w_query, w_kv, w_out):
    section_count = lax.axis_size("section")
    group_count = lax.axis_size("dp")
    section_index = lax.axis_index("section")
    tok_rows = hidden.shape[0]
    features = hidden.shape[1]
    block_count = neighbours.shape[0]
    nbr_length = neighbours.shape[1]
    local_cols = w_query.shape[2]
    heads_here = local_cols // DH
    micro_count = tok_rows // MB
    scaling = DH ** (-0.5)
    gain_row = norm_gain[0]
    query_weight = w_query[0]
    pair_weight = w_kv[0].reshape(features, 2 * local_cols)
    out_weight = w_out[0]
    pieces = lax.all_gather(neighbours, "dp", axis=0, tiled=True)
    flat_rows = pieces.reshape(-1, features)
    projected = jnp.dot(flat_rows, pair_weight, preferred_element_type=jnp.float32).astype(
        jnp.bfloat16
    )
    key_values = projected.reshape(pieces.shape[0], pieces.shape[1], 2 * local_cols)
    key_values = key_values.reshape(group_count, block_count, nbr_length, 2, heads_here, DH)

    def make_queries(pieces):
        widened = pieces.astype(jnp.float32)
        moment = jnp.mean(widened * widened, axis=-1, keepdims=True)
        normed = (widened * lax.rsqrt(moment + 1e-05) * gain_row).astype(jnp.bfloat16)
        return (jnp.dot(normed, query_weight, preferred_element_type=jnp.float32) * scaling).astype(
            jnp.bfloat16
        )

    def attend(queries_flat, clamped):
        queries = queries_flat.reshape(group_count, MB, heads_here, DH)
        block_index = clamped * MB // BLOCK_LEN
        key_block = lax.dynamic_index_in_dim(key_values, block_index, axis=1, keepdims=False)
        scores = jnp.einsum(
            "gqhe,gkhe->ghqk", queries, key_block[:, :, 0], preferred_element_type=jnp.float32
        )
        weights_soft = jax.nn.softmax(scores, axis=-1).astype(jnp.bfloat16)
        attended = jnp.einsum(
            "ghqk,gkhe->gqhe", weights_soft, key_block[:, :, 1], preferred_element_type=jnp.float32
        )
        return attended.astype(jnp.bfloat16).reshape(group_count * MB, local_cols)

    def head_output(attended):
        partial_term = jnp.dot(attended, out_weight, preferred_element_type=jnp.float32)
        return lax.psum_scatter(
            lax.optimization_barrier(partial_term.astype(jnp.bfloat16))
            .astype(jnp.float32)
            .astype(jnp.bfloat16),
            "dp",
            scatter_dimension=0,
            tiled=True,
        ).astype(jnp.float32)

    def record(outputs, updated_rows, micro_index, clamped):
        active = (micro_index >= 0) & (micro_index < micro_count)
        written = lax.dynamic_update_slice_in_dim(outputs, updated_rows, clamped * MB, 0)
        return jnp.where(active, written, outputs)

    def step_once(step_number, loop_state):
        incoming, outputs = loop_state
        micro_index = step_number - section_index
        clamped = jnp.clip(micro_index, 0, micro_count - 1)
        own_block = lax.dynamic_slice_in_dim(hidden, clamped * MB, MB, 0)
        current = jnp.where(section_index == 0, own_block, incoming)
        queries = make_queries(lax.all_gather(current, "dp", axis=0, tiled=True))
        branch = head_output(attend(queries, clamped))
        updated_rows = (current.astype(jnp.float32) + branch).astype(jnp.bfloat16)
        outputs = record(outputs, updated_rows, micro_index, clamped)
        incoming = passed_along(updated_rows, "section", 1)
        return (incoming, outputs)

    start_rows = jnp.zeros((MB, features), jnp.bfloat16)
    start_state = (start_rows, jnp.zeros((tok_rows, features), jnp.bfloat16))
    final_state = lax.fori_loop(0, micro_count + section_count - 1, step_once, start_state)
    return final_state[1][None]


def solution(mesh):
    placed = (
        P("dp", None),
        P("dp", None, None),
        P("section", None),
        P("section", None, "dp"),
        P("section", None, None, "dp"),
        P("section", "dp", None),
    )
    return jax.shard_map(
        per_device, mesh=mesh, in_specs=placed, out_specs=P("section", "dp", None), check_vma=False
    )
```

profile of v0, /device:TPU:7, one launch (start us, length us, event | category | flops | bytes accessed | tf_op | source)
XLA Modules:
  0.0 784.1 jit_solution(10541293016856759200)
XLA Ops:
  7.3 9.3 %copy.9 = bf16[512,8,2,512]{3,1,2,0:T(8,128)(2,1)} copy(bf16[512,8,2,512]{3,2,1,0:T(2,128)(2,1)} %bitcast.57) | data formatting | bytes 16777216
  16.6 76.0 %all-gather.2.cloned.1.call-done = bf16[8,128,4096]{2,1,0:T(8,128)(2,1)} async-done(((bf16[1,128,4096]{2,1,0:T(8,128)(2,1)}), bf16[8,128,4096]{2,1,0:T(8,128)(2,1)}) %all-gather.2.cloned.1.call-update) | async-done | bytes 8388624 | tf_op jit(solution)/shard_map/all_gather | solution.py:33
  92.6 13.7 %convolution_convert_fusion.2 = bf16[1024,1024]{1,0:T(8,128)(2,1)S(1)} fusion(bf16[1024,4096]{1,0:T(8,128)(2,1)} %bitcast.60, bf16[4096,1024]{1,0:T(8,128)(2,1)} %bitcast.58), kind=kOutput, calls=%fused_computation.27 | convolution fusion | flops 8590983168 | bytes 18874368 | tf_op jit(solution)/shard_map/dot_general | solution.py:35
  106.3 2.7 reshape_reshape.3
  109.0 2.1 copy.8
  111.2 665.2 %while.16 = (s32[]{:T(128)}, bf16[8,4096]{1,0:T(8,128)(2,1)S(1)}, bf16[64,4096]{1,0:T(8,128)(2,1)S(1)}, pred[]{:T(512)}, s32[]{:T(128)}, /*index=5*/bf16[64,4096...) while((s32[]{:T(128)}, bf16[8,4096]{1,0:T(8,128)(2,1)S(1)}, ...), condition=%wide.region_5.6_spmd, body=%wide.region_0.5_spmd.sunk | while | flops 556204608 | bytes 15764046 | solution.py:93
  112.2 14.9 %all_gather.13 = bf16[64,4096]{1,0:T(8,128)(2,1)S(1)} all-gather(bf16[8,4096]{1,0:T(8,128)(2,1)S(1)} %dynamic-slice_select_fusion.2), channel_id=1, replica_groups=mesh['section'=4,'dp'=8] {'dp'}, dimensions={0}, use_global_device_ids=true | all-gather | bytes 589824 | tf_op jit(solution)/shard_map/while/body/eval_jaxpr/all_gather | solution.py:84
  127.3 3.7 fusion.41
  131.2 4.2 convolution_convert_fusion.4
  135.5 26.1 %reduce-scatter.2.cloned.1.call-done = bf16[8,4096]{1,0:T(8,128)(2,1)} async-done(((bf16[64,4096]{1,0:T(8,128)(2,1)}), bf16[8,4096]{1,0:T(8,128)(2,1)}) %reduce-scatter.2.cloned.1.call-update) | async-done | bytes 65552 | tf_op jit(solution)/shard_map/while/body/eval_jaxpr/reduce_scatter | solution.py:64
  162.5 1.3 collective-permute-start
  163.8 3.7 collective-permute-done
  168.3 19.5 %all_gather.13 = bf16[64,4096]{1,0:T(8,128)(2,1)S(1)} all-gather(bf16[8,4096]{1,0:T(8,128)(2,1)S(1)} %dynamic-slice_select_fusion.2), channel_id=1, replica_groups=mesh['section'=4,'dp'=8] {'dp'}, dimensions={0}, use_global_device_ids=true | all-gather | bytes 589824 | tf_op jit(solution)/shard_map/while/body/eval_jaxpr/all_gather | solution.py:84
  188.0 3.7 fusion.41
  191.9 4.2 convolution_convert_fusion.4
  196.2 26.2 %reduce-scatter.2.cloned.1.call-done = bf16[8,4096]{1,0:T(8,128)(2,1)} async-done(((bf16[64,4096]{1,0:T(8,128)(2,1)}), bf16[8,4096]{1,0:T(8,128)(2,1)}) %reduce-scatter.2.cloned.1.call-update) | async-done | bytes 65552 | tf_op jit(solution)/shard_map/while/body/eval_jaxpr/reduce_scatter | solution.py:64
  223.3 1.3 collective-permute-start
  224.6 3.7 collective-permute-done
  229.2 19.5 %all_gather.13 = bf16[64,4096]{1,0:T(8,128)(2,1)S(1)} all-gather(bf16[8,4096]{1,0:T(8,128)(2,1)S(1)} %dynamic-slice_select_fusion.2), channel_id=1, replica_groups=mesh['section'=4,'dp'=8] {'dp'}, dimensions={0}, use_global_device_ids=true | all-gather | bytes 589824 | tf_op jit(solution)/shard_map/while/body/eval_jaxpr/all_gather | solution.py:84
  248.9 3.7 fusion.41
  252.8 4.2 convolution_convert_fusion.4
  257.0 26.3 %reduce-scatter.2.cloned.1.call-done = bf16[8,4096]{1,0:T(8,128)(2,1)} async-done(((bf16[64,4096]{1,0:T(8,128)(2,1)}), bf16[8,4096]{1,0:T(8,128)(2,1)}) %reduce-scatter.2.cloned.1.call-update) | async-done | bytes 65552 | tf_op jit(solution)/shard_map/while/body/eval_jaxpr/reduce_scatter | solution.py:64
  285.5 3.7 collective-permute-done
  290.0 19.5 %all_gather.13 = bf16[64,4096]{1,0:T(8,128)(2,1)S(1)} all-gather(bf16[8,4096]{1,0:T(8,128)(2,1)S(1)} %dynamic-slice_select_fusion.2), channel_id=1, replica_groups=mesh['section'=4,'dp'=8] {'dp'}, dimensions={0}, use_global_device_ids=true | all-gather | bytes 589824 | tf_op jit(solution)/shard_map/while/body/eval_jaxpr/all_gather | solution.py:84
  309.8 3.7 fusion.41
  313.7 4.2 convolution_convert_fusion.4
  317.9 26.3 %reduce-scatter.2.cloned.1.call-done = bf16[8,4096]{1,0:T(8,128)(2,1)} async-done(((bf16[64,4096]{1,0:T(8,128)(2,1)}), bf16[8,4096]{1,0:T(8,128)(2,1)}) %reduce-scatter.2.cloned.1.call-update) | async-done | bytes 65552 | tf_op jit(solution)/shard_map/while/body/eval_jaxpr/reduce_scatter | solution.py:64
  346.4 3.7 collective-permute-done
  350.9 19.8 %all_gather.13 = bf16[64,4096]{1,0:T(8,128)(2,1)S(1)} all-gather(bf16[8,4096]{1,0:T(8,128)(2,1)S(1)} %dynamic-slice_select_fusion.2), channel_id=1, replica_groups=mesh['section'=4,'dp'=8] {'dp'}, dimensions={0}, use_global_device_ids=true | all-gather | bytes 589824 | tf_op jit(solution)/shard_map/while/body/eval_jaxpr/all_gather | solution.py:84
  370.9 3.7 fusion.41
  374.8 4.2 convolution_convert_fusion.4
  379.0 26.0 %reduce-scatter.2.cloned.1.call-done = bf16[8,4096]{1,0:T(8,128)(2,1)} async-done(((bf16[64,4096]{1,0:T(8,128)(2,1)}), bf16[8,4096]{1,0:T(8,128)(2,1)}) %reduce-scatter.2.cloned.1.call-update) | async-done | bytes 65552 | tf_op jit(solution)/shard_map/while/body/eval_jaxpr/reduce_scatter | solution.py:64
  407.3 3.7 collective-permute-done
  411.8 19.5 %all_gather.13 = bf16[64,4096]{1,0:T(8,128)(2,1)S(1)} all-gather(bf16[8,4096]{1,0:T(8,128)(2,1)S(1)} %dynamic-slice_select_fusion.2), channel_id=1, replica_groups=mesh['section'=4,'dp'=8] {'dp'}, dimensions={0}, use_global_device_ids=true | all-gather | bytes 589824 | tf_op jit(solution)/shard_map/while/body/eval_jaxpr/all_gather | solution.py:84
  431.5 3.7 fusion.41
  435.4 4.2 convolution_convert_fusion.4
  439.7 26.5 %reduce-scatter.2.cloned.1.call-done = bf16[8,4096]{1,0:T(8,128)(2,1)} async-done(((bf16[64,4096]{1,0:T(8,128)(2,1)}), bf16[8,4096]{1,0:T(8,128)(2,1)}) %reduce-scatter.2.cloned.1.call-update) | async-done | bytes 65552 | tf_op jit(solution)/shard_map/while/body/eval_jaxpr/reduce_scatter | solution.py:64
  467.0 1.3 collective-permute-start
  468.3 3.7 collective-permute-done
  472.9 19.5 %all_gather.13 = bf16[64,4096]{1,0:T(8,128)(2,1)S(1)} all-gather(bf16[8,4096]{1,0:T(8,128)(2,1)S(1)} %dynamic-slice_select_fusion.2), channel_id=1, replica_groups=mesh['section'=4,'dp'=8] {'dp'}, dimensions={0}, use_global_device_ids=true | all-gather | bytes 589824 | tf_op jit(solution)/shard_map/while/body/eval_jaxpr/all_gather | solution.py:84
  492.6 3.7 fusion.41
  496.5 4.2 convolution_convert_fusion.4
  500.8 26.3 %reduce-scatter.2.cloned.1.call-done = bf16[8,4096]{1,0:T(8,128)(2,1)} async-done(((bf16[64,4096]{1,0:T(8,128)(2,1)}), bf16[8,4096]{1,0:T(8,128)(2,1)}) %reduce-scatter.2.cloned.1.call-update) | async-done | bytes 65552 | tf_op jit(solution)/shard_map/while/body/eval_jaxpr/reduce_scatter | solution.py:64
  529.2 3.7 collective-permute-done
  533.8 19.8 %all_gather.13 = bf16[64,4096]{1,0:T(8,128)(2,1)S(1)} all-gather(bf16[8,4096]{1,0:T(8,128)(2,1)S(1)} %dynamic-slice_select_fusion.2), channel_id=1, replica_groups=mesh['section'=4,'dp'=8] {'dp'}, dimensions={0}, use_global_device_ids=true | all-gather | bytes 589824 | tf_op jit(solution)/shard_map/while/body/eval_jaxpr/all_gather | solution.py:84
  553.8 3.7 fusion.41
  557.7 4.2 convolution_convert_fusion.4
  561.9 26.0 %reduce-scatter.2.cloned.1.call-done = bf16[8,4096]{1,0:T(8,128)(2,1)} async-done(((bf16[64,4096]{1,0:T(8,128)(2,1)}), bf16[8,4096]{1,0:T(8,128)(2,1)}) %reduce-scatter.2.cloned.1.call-update) | async-done | bytes 65552 | tf_op jit(solution)/shard_map/while/body/eval_jaxpr/reduce_scatter | solution.py:64
  590.1 3.7 collective-permute-done
  594.7 19.5 %all_gather.13 = bf16[64,4096]{1,0:T(8,128)(2,1)S(1)} all-gather(bf16[8,4096]{1,0:T(8,128)(2,1)S(1)} %dynamic-slice_select_fusion.2), channel_id=1, replica_groups=mesh['section'=4,'dp'=8] {'dp'}, dimensions={0}, use_global_device_ids=true | all-gather | bytes 589824 | tf_op jit(solution)/shard_map/while/body/eval_jaxpr/all_gather | solution.py:84
  614.4 3.7 fusion.41
  618.3 4.2 convolution_convert_fusion.4
  622.5 26.3 %reduce-scatter.2.cloned.1.call-done = bf16[8,4096]{1,0:T(8,128)(2,1)} async-done(((bf16[64,4096]{1,0:T(8,128)(2,1)}), bf16[8,4096]{1,0:T(8,128)(2,1)}) %reduce-scatter.2.cloned.1.call-update) | async-done | bytes 65552 | tf_op jit(solution)/shard_map/while/body/eval_jaxpr/reduce_scatter | solution.py:64
  651.0 3.7 collective-permute-done
  655.6 19.7 %all_gather.13 = bf16[64,4096]{1,0:T(8,128)(2,1)S(1)} all-gather(bf16[8,4096]{1,0:T(8,128)(2,1)S(1)} %dynamic-slice_select_fusion.2), channel_id=1, replica_groups=mesh['section'=4,'dp'=8] {'dp'}, dimensions={0}, use_global_device_ids=true | all-gather | bytes 589824 | tf_op jit(solution)/shard_map/while/body/eval_jaxpr/all_gather | solution.py:84
  675.5 3.7 fusion.41
  679.4 4.2 convolution_convert_fusion.4
  683.6 26.1 %reduce-scatter.2.cloned.1.call-done = bf16[8,4096]{1,0:T(8,128)(2,1)} async-done(((bf16[64,4096]{1,0:T(8,128)(2,1)}), bf16[8,4096]{1,0:T(8,128)(2,1)}) %reduce-scatter.2.cloned.1.call-update) | async-done | bytes 65552 | tf_op jit(solution)/shard_map/while/body/eval_jaxpr/reduce_scatter | solution.py:64
  711.9 3.7 collective-permute-done
  716.5 19.6 %all_gather.13 = bf16[64,4096]{1,0:T(8,128)(2,1)S(1)} all-gather(bf16[8,4096]{1,0:T(8,128)(2,1)S(1)} %dynamic-slice_select_fusion.2), channel_id=1, replica_groups=mesh['section'=4,'dp'=8] {'dp'}, dimensions={0}, use_global_device_ids=true | all-gather | bytes 589824 | tf_op jit(solution)/shard_map/while/body/eval_jaxpr/all_gather | solution.py:84
  736.3 3.7 fusion.41
  740.2 4.2 convolution_convert_fusion.4
  744.5 26.1 %reduce-scatter.2.cloned.1.call-done = bf16[8,4096]{1,0:T(8,128)(2,1)} async-done(((bf16[64,4096]{1,0:T(8,128)(2,1)}), bf16[8,4096]{1,0:T(8,128)(2,1)}) %reduce-scatter.2.cloned.1.call-update) | async-done | bytes 65552 | tf_op jit(solution)/shard_map/while/body/eval_jaxpr/reduce_scatter | solution.py:64
  772.7 3.7 collective-permute-done
  (93 shorter events, 36.0 us)
Async XLA Ops:
  6.5 86.0 %all-gather.2.cloned.1.call-start = ((), (), s32[]{:S(2)}) async-start(), calls=%async_computation.1 | async-start | bytes 9437184 | tf_op jit(solution)/shard_map/all_gather | solution.py:33
  106.2 5.0 copy-start.1
  111.2 50.4 %reduce-scatter.2.cloned.1.call-start = ((), (), s32[]{:S(2)}) async-start(), calls=%async_computation.2 | async-start | bytes 589824 | tf_op jit(solution)/shard_map/while/body/eval_jaxpr/reduce_scatter | solution.py:64
  162.5 5.0 collective-permute-start
  167.5 55.0 %reduce-scatter.2.cloned.1.call-start = ((), (), s32[]{:S(2)}) async-start(), calls=%async_computation.2 | async-start | bytes 589824 | tf_op jit(solution)/shard_map/while/body/eval_jaxpr/reduce_scatter | solution.py:64
  223.3 5.0 collective-permute-start
  228.3 55.0 %reduce-scatter.2.cloned.1.call-start = ((), (), s32[]{:S(2)}) async-start(), calls=%async_computation.2 | async-start | bytes 589824 | tf_op jit(solution)/shard_map/while/body/eval_jaxpr/reduce_scatter | solution.py:64
  284.2 5.0 collective-permute-start
  289.2 55.0 %reduce-scatter.2.cloned.1.call-start = ((), (), s32[]{:S(2)}) async-start(), calls=%async_computation.2 | async-start | bytes 589824 | tf_op jit(solution)/shard_map/while/body/eval_jaxpr/reduce_scatter | solution.py:64
  345.1 5.0 collective-permute-start
  350.1 55.0 %reduce-scatter.2.cloned.1.call-start = ((), (), s32[]{:S(2)}) async-start(), calls=%async_computation.2 | async-start | bytes 589824 | tf_op jit(solution)/shard_map/while/body/eval_jaxpr/reduce_scatter | solution.py:64
  406.0 5.0 collective-permute-start
  411.0 55.2 %reduce-scatter.2.cloned.1.call-start = ((), (), s32[]{:S(2)}) async-start(), calls=%async_computation.2 | async-start | bytes 589824 | tf_op jit(solution)/shard_map/while/body/eval_jaxpr/reduce_scatter | solution.py:64
  467.0 5.0 collective-permute-start
  472.0 55.0 %reduce-scatter.2.cloned.1.call-start = ((), (), s32[]{:S(2)}) async-start(), calls=%async_computation.2 | async-start | bytes 589824 | tf_op jit(solution)/shard_map/while/body/eval_jaxpr/reduce_scatter | solution.py:64
  527.9 5.0 collective-permute-start
  532.9 55.0 %reduce-scatter.2.cloned.1.call-start = ((), (), s32[]{:S(2)}) async-start(), calls=%async_computation.2 | async-start | bytes 589824 | tf_op jit(solution)/shard_map/while/body/eval_jaxpr/reduce_scatter | solution.py:64
  588.8 5.0 collective-permute-start
  593.8 55.0 %reduce-scatter.2.cloned.1.call-start = ((), (), s32[]{:S(2)}) async-start(), calls=%async_computation.2 | async-start | bytes 589824 | tf_op jit(solution)/shard_map/while/body/eval_jaxpr/reduce_scatter | solution.py:64
  649.7 5.0 collective-permute-start
  654.7 55.0 %reduce-scatter.2.cloned.1.call-start = ((), (), s32[]{:S(2)}) async-start(), calls=%async_computation.2 | async-start | bytes 589824 | tf_op jit(solution)/shard_map/while/body/eval_jaxpr/reduce_scatter | solution.py:64
  710.6 5.0 collective-permute-start
  715.6 54.9 %reduce-scatter.2.cloned.1.call-start = ((), (), s32[]{:S(2)}) async-start(), calls=%async_computation.2 | async-start | bytes 589824 | tf_op jit(solution)/shard_map/while/body/eval_jaxpr/reduce_scatter | solution.py:64
  771.4 5.0 collective-permute-start
  776.4 0.8 copy-start
Sparse Core Ops, SparseCore 0:
  8.9 83.6 all-gather.1
  135.6 25.9 reduce-scatter.1
  196.3 26.0 reduce-scatter.1
  257.1 26.1 reduce-scatter.1
  318.0 26.1 reduce-scatter.1
  379.2 25.8 reduce-scatter.1
  439.8 26.3 reduce-scatter.1
  500.9 26.1 reduce-scatter.1
  562.0 25.8 reduce-scatter.1
  622.6 26.1 reduce-scatter.1
  683.7 25.9 reduce-scatter.1
  744.6 25.9 reduce-scatter.1
where the time goes:
time: 791 us; the launch traced here: 784 us
  waiting for transfers between devices  406 us (51%)
  blocking collectives  211 us (27%)
  matrix products  100 us (13%)
  other arithmetic  23.8 us (3%)
  local copies, waits for them, and re-layouts  15 us (2%)
  starting transfers between devices  14.3 us (2%)
  between operations  13.4 us (2%)
    reduce_scatter x11, waiting for transfers between devices, head_output(): lax.psum_scatter(lax.optimization_barrier(partial_term.astype(jnp.bfloat1...  288 us
    all_gather x11, blocking collectives, step_once(): queries = make_queries(lax.all_gather(current, 'dp', axis=0, tiled=True))  211 us
    all_gather x1, waiting for transfers between devices, per_device(): pieces = lax.all_gather(neighbours, 'dp', axis=0, tiled=True)  76 us
    dot_general x11, matrix products, head_output(): jnp.dot(attended, out_weight, preferred_element_type=jnp.float32)  46.3 us
    ppermute x11, waiting for transfers between devices, passed_along(): return lax.ppermute(block, axis, route)  40.8 us
    dot_general x11, matrix products, attend(): jnp.einsum('gqhe,gkhe->ghqk', queries, key_block[:, :, 0], preferred_elem...  40.4 us
  transfers between devices with their start and end apart: 23, of which 23 were waited for; matrix products, arithmetic and copies ran while one was open for 1% of the time, Pallas kernels for 0%

commit v1 on v0

v1 whole, which is shorter than its diff:
```python
import functools
import jax
import jax.numpy as jnp
from jax import lax
from jax.experimental import pallas as pl
from jax.experimental.pallas import tpu as pltpu
from jax.sharding import PartitionSpec as P

DH = 128
BLOCK_LEN = 64
MB = 16
CHUNKS = 2
F32 = jnp.float32
BF16 = jnp.bfloat16


def remote(src, dst, send_sem, recv_sem, section, dp):
    return pltpu.make_async_remote_copy(
        src_ref=src,
        dst_ref=dst,
        send_sem=send_sem,
        recv_sem=recv_sem,
        device_id=(section, dp),
        device_id_type=pl.DeviceIdType.MESH,
    )


def relay_kernel(
    sections,
    group,
    hidden_hbm,
    gain_ref,
    wq_hbm,
    kv_ref,
    wo_hbm,
    out_ref,
    wq,
    wo,
    hbuf,
    gbuf,
    pbuf,
    r1,
    tsum,
    r2,
    load_sem,
    h_send,
    h_recv,
    g_send,
    g_recv,
    f_send,
    f_recv,
    r1_send,
    r1_recv,
    r2_send,
    r2_recv,
):
    section = lax.axis_index("section")
    me = lax.axis_index("dp")
    chips = group // 2
    core = me % 2
    chip = me // 2
    other = 1 - core
    sibling = chip * 2 + other
    micro_count, mb, features = hbuf.shape
    cols = wq.shape[1]
    heads = cols // DH
    per_dev = kv_ref.shape[0] // group
    width = features // CHUNKS
    scaling = DH ** (-0.5)

    def peer(k):
        return ((chip + k) % chips) * 2 + core

    def source_chip(k):
        return (chip + chips - k) % chips

    wq_load = pltpu.make_async_copy(wq_hbm, wq, load_sem.at[0])
    wo_load = pltpu.make_async_copy(wo_hbm, wo, load_sem.at[1])
    wq_load.start()
    wo_load.start()
    h_load = pltpu.make_async_copy(hidden_hbm, hbuf, load_sem.at[2])

    @pl.when(section == 0)
    def _():
        h_load.start()

    barrier = pltpu.get_barrier_semaphore()

    def greet(s, d):
        pl.semaphore_signal(
            barrier, inc=1, device_id=(s, d), device_id_type=pl.DeviceIdType.MESH
        )

    greet(section, sibling)
    for k in range(1, chips):
        greet(section, peer(k))

    greet((section + 1) % sections, me)
    greet((section + sections - 1) % sections, me)
    pl.semaphore_wait(barrier, chips + 2)

    @pl.when(section == 0)
    def _():
        h_load.wait()

    def h_copy(m):
        return remote(
            out_ref.at[m], hbuf.at[m], h_send.at[m], h_recv.at[m], (section + 1) % sections, me
        )

    def g_copy(m, k):
        slot = gbuf.at[m, me]
        target = sibling if k == 0 else peer(k)
        return remote(slot, slot, g_send.at[m, k], g_recv.at[m, k], section, target)

    def g_arrival(m, k):
        source = sibling if k == 0 else source_chip(k) * 2 + core
        slot = gbuf.at[m, source]
        return remote(slot, slot, g_send.at[m, k], g_recv.at[m, k], section, sibling)

    def f_copy(m, k):
        slot = gbuf.at[m, source_chip(k) * 2 + core]
        return remote(slot, slot, f_send.at[m, k], f_recv.at[m, k], section, sibling)

    def f_arrival(m, k):
        slot = gbuf.at[m, source_chip(k) * 2 + other]
        return remote(slot, slot, f_send.at[m, k], f_recv.at[m, k], section, sibling)

    def r1_copy(m, j):
        return remote(
            pbuf.at[m, other, :, :, pl.ds(j * width, width)],
            r1.at[m, :, :, pl.ds(j * width, width)],
            r1_send.at[m, j],
            r1_recv.at[m, j],
            section,
            sibling,
        )

    def r2_copy(m, j, k):
        return remote(
            tsum.at[m, k, :, pl.ds(j * width, width)],
            r2.at[m, k, :, pl.ds(j * width, width)],
            r2_send.at[m, j, k],
            r2_recv.at[m, j, k],
            section,
            peer(k),
        )

    def begin(m):
        @pl.when(section > 0)
        def _():
            h_copy(m).wait_recv()

        x = hbuf[m].astype(F32)
        moment = jnp.mean(x * x, axis=-1, keepdims=True)
        gbuf[m, me] = (x * lax.rsqrt(moment + 1e-05) * gain_ref[...]).astype(BF16)
        for k in range(1, chips):
            g_copy(m, k).start()
        g_copy(m, 0).start()

    def pass_on(m):
        for k in range(1, chips):
            g_arrival(m, k).wait_recv()
            f_copy(m, k).start()

    def compute(m):
        g_arrival(m, 0).wait_recv()
        for k in range(1, chips):
            f_arrival(m, k).wait_recv()
        x = gbuf[m].reshape(group * mb, features)
        q = (jnp.dot(x, wq[...], preferred_element_type=F32) * scaling).astype(BF16)
        block = (m * mb) // BLOCK_LEN
        heads_out = []
        for h in range(heads):
            ks = slice(h * DH, (h + 1) * DH)
            vs = slice(cols + h * DH, cols + (h + 1) * DH)
            scores = jnp.concatenate(
                [
                    lax.dot_general(
                        q[n * mb : (n + 1) * mb, ks],
                        kv_ref[n * per_dev + block, :, ks],
                        (((1,), (1,)), ((), ())),
                        preferred_element_type=F32,
                    )
                    for n in range(group)
                ],
                axis=0,
            )
            e = jnp.exp(scores - jnp.max(scores, axis=-1, keepdims=True))
            probs = (e / jnp.sum(e, axis=-1, keepdims=True)).astype(BF16)
            heads_out.append(
                jnp.concatenate(
                    [
                        jnp.dot(
                            probs[n * mb : (n + 1) * mb],
                            kv_ref[n * per_dev + block, :, vs],
                            preferred_element_type=F32,
                        )
                        for n in range(group)
                    ],
                    axis=0,
                ).astype(BF16)
            )
        attended = jnp.concatenate(heads_out, axis=1)
        for j in range(CHUNKS):
            at = slice(j * width, (j + 1) * width)
            part = jnp.dot(attended, wo[:, at], preferred_element_type=F32).astype(BF16)
            for n in range(group):
                pbuf[m, n % 2, n // 2, :, at] = part[n * mb : (n + 1) * mb]
            r1_copy(m, j).start()

    def exchange(m):
        for j in range(CHUNKS):
            at = slice(j * width, (j + 1) * width)
            r1_copy(m, j).wait_recv()
            for k in range(1, chips):
                c = (chip + k) % chips
                tsum[m, k, :, at] = (
                    pbuf[m, core, c, :, at].astype(F32) + r1[m, c, :, at].astype(F32)
                ).astype(BF16)
                r2_copy(m, j, k).start()

    def finish(m):
        for j in range(CHUNKS):
            at = slice(j * width, (j + 1) * width)
            total = hbuf[m, :, at].astype(F32)
            total += pbuf[m, core, chip, :, at].astype(F32) + r1[m, chip, :, at].astype(F32)
            for k in range(1, chips):
                r2_copy(m, j, k).wait_recv()
                total += r2[m, k, :, at].astype(F32)
            out_ref[m, :, at] = total.astype(BF16)

        @pl.when(section < sections - 1)
        def _():
            h_copy(m).start()

    begin(0)
    wq_load.wait()
    wo_load.wait()
    pass_on(0)

    def step(m, carry):
        compute(m)

        @pl.when(m + 1 < micro_count)
        def _():
            begin(m + 1)

        exchange(m)

        @pl.when(m + 1 < micro_count)
        def _():
            pass_on(m + 1)

        finish(m)
        return carry

    lax.fori_loop(0, micro_count, step, 0)

    def drain(m, carry):
        for k in range(chips):
            g_copy(m, k).wait_send()
        for k in range(1, chips):
            f_copy(m, k).wait_send()
        for j in range(CHUNKS):
            r1_copy(m, j).wait_send()
            for k in range(1, chips):
                r2_copy(m, j, k).wait_send()

        @pl.when(section < sections - 1)
        def _():
            h_copy(m).wait_send()

        return carry

    lax.fori_loop(0, micro_count, drain, 0)


def per_device(sections, group, hidden, neighbours, norm_gain, w_query, w_kv, w_out):
    tok_rows, features = hidden.shape
    block_count, nbr_length = neighbours.shape[:2]
    cols = w_query.shape[2]
    micro = tok_rows // MB
    chips = group // 2
    pair_weight = w_kv[0].reshape(features, 2 * cols)
    pieces = lax.all_gather(neighbours, "dp", axis=0, tiled=True)
    projected = jnp.dot(
        pieces.reshape(-1, features), pair_weight, preferred_element_type=F32
    ).astype(BF16)
    key_values = projected.reshape(group * block_count, nbr_length, 2 * cols)
    dma = pltpu.SemaphoreType.DMA
    anywhere = pl.BlockSpec(memory_space=pl.ANY)
    vmem = pl.BlockSpec(memory_space=pltpu.VMEM)
    out = pl.pallas_call(
        functools.partial(relay_kernel, sections, group),
        out_shape=jax.ShapeDtypeStruct((micro, MB, features), BF16),
        in_specs=[anywhere, vmem, anywhere, vmem, anywhere],
        out_specs=vmem,
        scratch_shapes=[
            pltpu.VMEM((features, cols), BF16),
            pltpu.VMEM((cols, features), BF16),
            pltpu.VMEM((micro, MB, features), BF16),
            pltpu.VMEM((micro, group, MB, features), BF16),
            pltpu.VMEM((micro, 2, chips, MB, features), BF16),
            pltpu.VMEM((micro, chips, MB, features), BF16),
            pltpu.VMEM((micro, chips, MB, features), BF16),
            pltpu.VMEM((micro, chips, MB, features), BF16),
            dma((3,)),
            dma((micro,)),
            dma((micro,)),
            dma((micro, chips)),
            dma((micro, chips)),
            dma((micro, chips)),
            dma((micro, chips)),
            dma((micro, CHUNKS)),
            dma((micro, CHUNKS)),
            dma((micro, CHUNKS, chips)),
            dma((micro, CHUNKS, chips)),
        ],
        compiler_params=pltpu.CompilerParams(
            collective_id=0, has_side_effects=True, vmem_limit_bytes=60 * 1024 * 1024
        ),
    )(hidden.reshape(micro, MB, features), norm_gain, w_query[0], key_values, w_out[0])
    return out.reshape(1, tok_rows, features)


def solution(mesh):
    placed = (
        P("dp", None),
        P("dp", None, None),
        P("section", None),
        P("section", None, "dp"),
        P("section", None, None, "dp"),
        P("section", "dp", None),
    )
    body = functools.partial(per_device, mesh.shape["section"], mesh.shape["dp"])
    return jax.shard_map(
        body, mesh=mesh, in_specs=placed, out_specs=P("section", "dp", None), check_vma=False
    )
```

time: 791 us -> 387 us (0.49)
  waiting for transfers between devices: 406 us -> 76.7 us
  Pallas kernels: 0 us -> 271 us
  blocking collectives: 211 us -> 0 us
  matrix products: 100 us -> 14.7 us
  other arithmetic: 23.8 us -> 0 us
  starting transfers between devices: 14.3 us -> 0.01 us
    reduce_scatter x11 -> x0, waiting for transfers between devices: 288 us -> none  [head_output(): lax.psum_scatter(lax.optimization_barrier(partial_term.astype(jnp.bfloat1...]
    pallas_call x0 -> x1, Pallas kernels: none -> 271 us  [per_device(): pl.pallas_call(functools.partial(relay_kernel, sections, group), out_shap...]
    all_gather x11 -> x0, blocking collectives: 211 us -> none  [step_once(): queries = make_queries(lax.all_gather(current, 'dp', axis=0, tiled=True))]
    dot_general x23 -> x1, matrix products: 100 us -> 14.7 us  [per_device(): jnp.dot(pieces.reshape(-1, features), pair_weight, preferred_element_type...]
    ppermute x11 -> x0, waiting for transfers between devices: 40.8 us -> none  [passed_along(): return lax.ppermute(block, axis, route)]
    select_n x22 -> x0, other arithmetic: 19 us -> none  [the longest x11 9.55 us: record(): return jnp.where(active, written, outputs)]
    ppermute x11 -> x0, starting transfers between devices: 14.2 us -> none  [passed_along(): return lax.ppermute(block, axis, route)]
  transfers between devices with their start and end apart: 23 -> 1, of which waited for: 23 -> 1; matrix products, arithmetic and copies ran while one was open for 1% -> 2% of each run, Pallas kernels for 0% -> 0%
where the time goes in v1:
time: 387 us
  Pallas kernels  271 us (70%)
  waiting for transfers between devices  76.7 us (20%)
  matrix products  14.7 us (4%)
  between operations  13.4 us (3%)
  local copies, waits for them, and re-layouts  11.2 us (3%)
    pallas_call x1, Pallas kernels, per_device(): pl.pallas_call(functools.partial(relay_kernel, sections, group), out_shap...  271 us
    all_gather x1, waiting for transfers between devices, per_device(): pieces = lax.all_gather(neighbours, 'dp', axis=0, tiled=True)  76 us
    dot_general x1, matrix products, per_device(): jnp.dot(pieces.reshape(-1, features), pair_weight, preferred_element_type...  14.7 us
    unnamed x2, local copies, waits for them, and re-layouts  11.2 us
  transfers between devices with their start and end apart: 1, of which 1 were waited for; matrix products, arithmetic and copies ran while one was open for 2% of the time, Pallas kernels for 0%

profile of v1, /device:TPU:7, one launch (start us, length us, event | category | flops | bytes accessed | tf_op | source)
XLA Modules:
  0.0 387.1 jit_solution(6064240906469900040)
XLA Ops:
  6.5 0.0 all-gather.2.cloned.1.call-start
  6.5 0.7 all-gather.2.cloned.1.call-update
  7.3 9.3 %copy.7 = bf16[512,8,2,512]{3,1,2,0:T(8,128)(2,1)} copy(bf16[512,8,2,512]{3,2,1,0:T(2,128)(2,1)} %bitcast.11) | data formatting | bytes 16777216
  16.6 76.0 %all-gather.2.cloned.1.call-done = bf16[8,128,4096]{2,1,0:T(8,128)(2,1)} async-done(((bf16[1,128,4096]{2,1,0:T(8,128)(2,1)}), bf16[8,128,4096]{2,1,0:T(8,128)(2,1)}) %all-gather.2.cloned.1.call-update) | async-done | bytes 8388624 | tf_op jit(solution)/shard_map/all_gather | solution.py:286
  92.6 14.7 %convolution_convert_fusion = bf16[1024,1024]{1,0:T(8,128)(2,1)} fusion(bf16[1024,4096]{1,0:T(8,128)(2,1)} %bitcast.18, bf16[4096,1024]{1,0:T(8,128)(2,1)} %bitcast.12), kind=kOutput, calls=%fused_computation | convolution fusion | flops 8590983168 | bytes 18874368 | tf_op jit(solution)/shard_map/dot_general | solution.py:287
  107.3 271.1 %shard_map.64 = bf16[4,16,4096]{2,1,0:T(8,128)(2,1)} custom-call(bf16[4,16,4096]{2,1,0:T(8,128)(2,1)} %bitcast.17, f32[1,4096]{1,0:T(1,128)} %gain_ref.1, bf16[4096,512]{1,0:T(8,128)(2,1)} %bitcast.13, bf16[8,128,1024]{2,1,0:T(8,128)(2,1)} %bitcast.16, bf16[512,4096]{1,0:T(8,128)(2,1)} %bitcast.14), custom_call_target="tpu_custom_call" | custom-call | tf_op jit(solution)/shard_map/pallas_call | solution.py:294
  378.3 1.9 copy.9
Async XLA Ops:
  6.5 86.0 %all-gather.2.cloned.1.call-start = ((), (), s32[]{:S(2)}) async-start(), calls=%async_computation | async-start | bytes 9437184 | tf_op jit(solution)/shard_map/all_gather | solution.py:286
Sparse Core Ops, SparseCore 0:
  8.9 83.6 all-gather.1

commit v2 on v1

--- a/solution.py
+++ b/solution.py
@@ -31,11 +31,15 @@
     hidden_hbm,
     gain_ref,
     wq_hbm,
-    kv_ref,
+    nbr_hbm,
+    wkv_hbm,
     wo_hbm,
     out_ref,
     wq,
     wo,
+    wkv,
+    nbuf,
+    kv_ref,
     hbuf,
     gbuf,
     pbuf,
@@ -43,6 +47,13 @@
     tsum,
     r2,
     load_sem,
+    n0_sem,
+    n1_send,
+    n1_recv,
+    n2_send,
+    n2_recv,
+    n3_send,
+    n3_recv,
     h_send,
     h_recv,
     g_send,
@@ -64,7 +75,8 @@
     micro_count, mb, features = hbuf.shape
     cols = wq.shape[1]
     heads = cols // DH
-    per_dev = kv_ref.shape[0] // group
+    blocks, nbr_length = kv_ref.shape[2:4]
+    pieces = nbuf.shape[2]
     width = features // CHUNKS
     scaling = DH ** (-0.5)
 
@@ -76,6 +88,10 @@
 
     wq_load = pltpu.make_async_copy(wq_hbm, wq, load_sem.at[0])
     wo_load = pltpu.make_async_copy(wo_hbm, wo, load_sem.at[1])
+    wkv_load = pltpu.make_async_copy(wkv_hbm, wkv, load_sem.at[3])
+    n_load = pltpu.make_async_copy(nbr_hbm, nbuf.at[chip, core], load_sem.at[4])
+    n_load.start()
+    wkv_load.start()
     wq_load.start()
     wo_load.start()
     h_load = pltpu.make_async_copy(hidden_hbm, hbuf, load_sem.at[2])
@@ -95,13 +111,80 @@
     for k in range(1, chips):
         greet(section, peer(k))
 
-    greet((section + 1) % sections, me)
-    greet((section + sections - 1) % sections, me)
-    pl.semaphore_wait(barrier, chips + 2)
-
-    @pl.when(section == 0)
-    def _():
-        h_load.wait()
+    for j in range(1, sections):
+        greet((section + j) % sections, me)
+    pl.semaphore_wait(barrier, chips + sections - 1)
+
+    def n0_copy():
+        return remote(
+            nbr_hbm, nbuf.at[chip, core], n0_sem.at[0], n0_sem.at[1], section, sibling
+        )
+
+    def n0_arrival():
+        slot = nbuf.at[chip, other]
+        return remote(slot, slot, n0_sem.at[0], n0_sem.at[1], section, sibling)
+
+    def n1_copy(k):
+        return remote(
+            nbr_hbm.at[section],
+            nbuf.at[chip, core, section],
+            n1_send.at[k],
+            n1_recv.at[k],
+            section,
+            peer(k),
+        )
+
+    def n1_arrival(k):
+        slot = nbuf.at[source_chip(k), core, section]
+        return remote(slot, slot, n1_send.at[k], n1_recv.at[k], section, sibling)
+
+    def n2_copy(k, j):
+        slot = nbuf.at[source_chip(k), core, section]
+        return remote(
+            slot, slot, n2_send.at[k, j], n2_recv.at[k, j], (section + j) % sections, me
+        )
+
+    def n2_arrival(k, j):
+        slot = nbuf.at[source_chip(k), core, (section + sections - j) % sections]
+        return remote(slot, slot, n2_send.at[k, j], n2_recv.at[k, j], section, sibling)
+
+    def n3_copy(k, j):
+        slot = nbuf.at[source_chip(k), core, (section + sections - j) % sections]
+        return remote(slot, slot, n3_send.at[k, j], n3_recv.at[k, j], section, sibling)
+
+    def n3_arrival(k, j):
+        slot = nbuf.at[source_chip(k), other, (section + sections - j) % sections]
+        return remote(slot, slot, n3_send.at[k, j], n3_recv.at[k, j], section, sibling)
+
+    def project(k):
+        c = source_chip(k)
+        if k == 0:
+            n_load.wait()
+            n0_arrival().wait_recv()
+        else:
+            for j in range(pieces):
+                n3_arrival(k, j).wait_recv()
+        tile = min(cols, 256)
+
+        def columns(i, carry):
+            at = pl.ds(pl.multiple_of(i * tile, tile), tile)
+            rows = nbuf[c].reshape(-1, features)
+            out = jnp.dot(rows, wkv[:, at], preferred_element_type=F32).astype(BF16)
+            kv_ref[c, :, :, :, at] = out.reshape(2, blocks, nbr_length, tile)
+            return carry
+
+        lax.fori_loop(0, 2 * cols // tile, columns, 0)
+
+    def spread(k):
+        n1_arrival(k).wait_recv()
+        for j in range(1, pieces):
+            n2_copy(k, j).start()
+        n3_copy(k, 0).start()
+
+    def share(k):
+        for j in range(1, pieces):
+            n2_arrival(k, j).wait_recv()
+            n3_copy(k, j).start()
 
     def h_copy(m):
         return remote(
@@ -169,7 +252,7 @@
             f_arrival(m, k).wait_recv()
         x = gbuf[m].reshape(group * mb, features)
         q = (jnp.dot(x, wq[...], preferred_element_type=F32) * scaling).astype(BF16)
-        block = (m * mb) // BLOCK_LEN
+        block = 0 if blocks == 1 else (m * mb) // BLOCK_LEN
         heads_out = []
         for h in range(heads):
             ks = slice(h * DH, (h + 1) * DH)
@@ -178,7 +261,7 @@
                 [
                     lax.dot_general(
                         q[n * mb : (n + 1) * mb, ks],
-                        kv_ref[n * per_dev + block, :, ks],
+                        kv_ref[n // 2, n % 2, block, :, ks],
                         (((1,), (1,)), ((), ())),
                         preferred_element_type=F32,
                     )
@@ -193,7 +276,7 @@
                     [
                         jnp.dot(
                             probs[n * mb : (n + 1) * mb],
-                            kv_ref[n * per_dev + block, :, vs],
+                            kv_ref[n // 2, n % 2, block, :, vs],
                             preferred_element_type=F32,
                         )
                         for n in range(group)
@@ -234,7 +317,32 @@
         def _():
             h_copy(m).start()
 
-    begin(0)
+    for k in range(1, chips):
+        n1_copy(k).start()
+    n0_copy().start()
+
+    @pl.when(section == 0)
+    def _():
+        h_load.wait()
+        begin(0)
+
+    wkv_load.wait()
+    spread(1)
+    for k in range(2, chips):
+        spread(k)
+        if k == 2:
+            project(0)
+        share(k - 1)
+    if chips == 2:
+        project(0)
+    share(chips - 1)
+    for k in range(1, chips):
+        project(k)
+
+    @pl.when(section > 0)
+    def _():
+        begin(0)
+
     wq_load.wait()
     wo_load.wait()
     pass_on(0)
@@ -242,20 +350,29 @@
     def step(m, carry):
         compute(m)
 
+        exchange(m)
+
         @pl.when(m + 1 < micro_count)
         def _():
             begin(m + 1)
 
-        exchange(m)
+        finish(m)
 
         @pl.when(m + 1 < micro_count)
         def _():
             pass_on(m + 1)
 
-        finish(m)
         return carry
 
     lax.fori_loop(0, micro_count, step, 0)
+
+    n0_copy().wait_send()
+    for k in range(1, chips):
+        n1_copy(k).wait_send()
+        for j in range(pieces):
+            n3_copy(k, j).wait_send()
+            if j > 0:
+                n2_copy(k, j).wait_send()
 
     def drain(m, carry):
         for k in range(chips):
@@ -283,29 +400,35 @@
     micro = tok_rows // MB
     chips = group // 2
     pair_weight = w_kv[0].reshape(features, 2 * cols)
-    pieces = lax.all_gather(neighbours, "dp", axis=0, tiled=True)
-    projected = jnp.dot(
-        pieces.reshape(-1, features), pair_weight, preferred_element_type=F32
-    ).astype(BF16)
-    key_values = projected.reshape(group * block_count, nbr_length, 2 * cols)
+    piece_rows = block_count * nbr_length // sections
     dma = pltpu.SemaphoreType.DMA
     anywhere = pl.BlockSpec(memory_space=pl.ANY)
     vmem = pl.BlockSpec(memory_space=pltpu.VMEM)
     out = pl.pallas_call(
         functools.partial(relay_kernel, sections, group),
         out_shape=jax.ShapeDtypeStruct((micro, MB, features), BF16),
-        in_specs=[anywhere, vmem, anywhere, vmem, anywhere],
+        in_specs=[anywhere, vmem, anywhere, anywhere, anywhere, anywhere],
         out_specs=vmem,
         scratch_shapes=[
             pltpu.VMEM((features, cols), BF16),
             pltpu.VMEM((cols, features), BF16),
+            pltpu.VMEM((features, 2 * cols), BF16),
+            pltpu.VMEM((chips, 2, sections, piece_rows, features), BF16),
+            pltpu.VMEM((chips, 2, block_count, nbr_length, 2 * cols), BF16),
             pltpu.VMEM((micro, MB, features), BF16),
             pltpu.VMEM((micro, group, MB, features), BF16),
             pltpu.VMEM((micro, 2, chips, MB, features), BF16),
             pltpu.VMEM((micro, chips, MB, features), BF16),
             pltpu.VMEM((micro, chips, MB, features), BF16),
             pltpu.VMEM((micro, chips, MB, features), BF16),
-            dma((3,)),
+            dma((5,)),
+            dma((2,)),
+            dma((chips,)),
+            dma((chips,)),
+            dma((chips, sections)),
+            dma((chips, sections)),
+            dma((chips, sections)),
+            dma((chips, sections)),
             dma((micro,)),
             dma((micro,)),
             dma((micro, chips)),
@@ -318,9 +441,16 @@
             dma((micro, CHUNKS, chips)),
         ],
         compiler_params=pltpu.CompilerParams(
-            collective_id=0, has_side_effects=True, vmem_limit_bytes=60 * 1024 * 1024
+            collective_id=0, has_side_effects=True, vmem_limit_bytes=62 * 1024 * 1024
         ),
-    )(hidden.reshape(micro, MB, features), norm_gain, w_query[0], key_values, w_out[0])
+    )(
+        hidden.reshape(micro, MB, features),
+        norm_gain,
+        w_query[0],
+        neighbours.reshape(sections, piece_rows, features),
+        pair_weight,
+        w_out[0],
+    )
     return out.reshape(1, tok_rows, features)
 
 

time: 387 us -> 283 us (0.73)
  waiting for transfers between devices: 76.7 us -> 0 us
  matrix products: 14.7 us -> 0 us
  between operations: 13.4 us -> 0.01 us
    all_gather x1 -> x0, waiting for transfers between devices: 76 us -> none  [per_device(): pieces = lax.all_gather(neighbours, 'dp', axis=0, tiled=True)]
    dot_general x1 -> x0, matrix products: 14.7 us -> none  [per_device(): jnp.dot(pieces.reshape(-1, features), pair_weight, preferred_element_type...]
  transfers between devices with their start and end apart: 1 -> 0, of which waited for: 1 -> 0; matrix products, arithmetic and copies ran while one was open for 2% -> 0% of each run, Pallas kernels for 0% -> 0%
where the time goes in v2:
time: 283 us; the launch traced here: 280 us
  Pallas kernels  269 us (95%)
  local copies, waits for them, and re-layouts  11.2 us (4%)
    pallas_call x1, Pallas kernels, per_device(): pl.pallas_call(functools.partial(relay_kernel, sections, group), out_shap...  269 us
    unnamed x2, local copies, waits for them, and re-layouts  11.2 us

profile of v2, /device:TPU:7, one launch (start us, length us, event | category | flops | bytes accessed | tf_op | source)
XLA Modules:
  0.0 279.9 jit_solution(17181619736144918536)
XLA Ops:
  0.0 9.3 %copy.7 = bf16[512,8,2,512]{3,1,2,0:T(8,128)(2,1)} copy(bf16[512,8,2,512]{3,2,1,0:T(2,128)(2,1)} %bitcast.9) | data formatting | bytes 16777216
  9.3 268.7 %shard_map.64 = bf16[4,16,4096]{2,1,0:T(8,128)(2,1)} custom-call(bf16[4,16,4096]{2,1,0:T(8,128)(2,1)} %bitcast.14, f32[1,4096]{1,0:T(1,128)} %gain_ref.1, bf16[4096,512]{1,0:T(8,128)(2,1)} %bitcast.10, bf16[4,32,4096]{2,1,0:T(8,128)(2,1)} %bitcast.13, bf16[4096,1024]{1,0:T(8,128)(2,1)} %bitcast.8, bf16[512,4096]{1,0:T(8,128)(2,1)} %bitcast.11), custom_call_target="tpu_custom_call" | custom-call | tf_op jit(solution)/shard_map/pallas_call | solution.py:407
  278.0 1.9 copy.9

commit v3 on v2

--- a/solution.py
+++ b/solution.py
@@ -191,23 +191,25 @@
             out_ref.at[m], hbuf.at[m], h_send.at[m], h_recv.at[m], (section + 1) % sections, me
         )
 
-    def g_copy(m, k):
-        slot = gbuf.at[m, me]
+    def g_slot(m, j, source):
+        return gbuf.at[m, source, :, pl.ds(j * width, width)]
+
+    def g_copy(m, j, k):
+        slot = g_slot(m, j, me)
         target = sibling if k == 0 else peer(k)
-        return remote(slot, slot, g_send.at[m, k], g_recv.at[m, k], section, target)
-
-    def g_arrival(m, k):
-        source = sibling if k == 0 else source_chip(k) * 2 + core
-        slot = gbuf.at[m, source]
-        return remote(slot, slot, g_send.at[m, k], g_recv.at[m, k], section, sibling)
-
-    def f_copy(m, k):
-        slot = gbuf.at[m, source_chip(k) * 2 + core]
-        return remote(slot, slot, f_send.at[m, k], f_recv.at[m, k], section, sibling)
-
-    def f_arrival(m, k):
-        slot = gbuf.at[m, source_chip(k) * 2 + other]
-        return remote(slot, slot, f_send.at[m, k], f_recv.at[m, k], section, sibling)
+        return remote(slot, slot, g_send.at[m, j, k], g_recv.at[m, j, k], section, target)
+
+    def g_arrival(m, j, k):
+        slot = g_slot(m, j, sibling if k == 0 else source_chip(k) * 2 + core)
+        return remote(slot, slot, g_send.at[m, j, k], g_recv.at[m, j, k], section, sibling)
+
+    def f_copy(m, j, k):
+        slot = g_slot(m, j, source_chip(k) * 2 + core)
+        return remote(slot, slot, f_send.at[m, j, k], f_recv.at[m, j, k], section, sibling)
+
+    def f_arrival(m, j, k):
+        slot = g_slot(m, j, source_chip(k) * 2 + other)
+        return remote(slot, slot, f_send.at[m, j, k], f_recv.at[m, j, k], section, sibling)
 
     def r1_copy(m, j):
         return remote(
@@ -237,21 +239,29 @@
         x = hbuf[m].astype(F32)
         moment = jnp.mean(x * x, axis=-1, keepdims=True)
         gbuf[m, me] = (x * lax.rsqrt(moment + 1e-05) * gain_ref[...]).astype(BF16)
+        for j in range(CHUNKS):
+            for k in range(1, chips):
+                g_copy(m, j, k).start()
+            g_copy(m, j, 0).start()
+
+    def pass_on(m, j=0):
         for k in range(1, chips):
-            g_copy(m, k).start()
-        g_copy(m, 0).start()
-
-    def pass_on(m):
-        for k in range(1, chips):
-            g_arrival(m, k).wait_recv()
-            f_copy(m, k).start()
+            g_arrival(m, j, k).wait_recv()
+            f_copy(m, j, k).start()
 
     def compute(m):
-        g_arrival(m, 0).wait_recv()
-        for k in range(1, chips):
-            f_arrival(m, k).wait_recv()
-        x = gbuf[m].reshape(group * mb, features)
-        q = (jnp.dot(x, wq[...], preferred_element_type=F32) * scaling).astype(BF16)
+        q = None
+        for j in range(CHUNKS):
+            g_arrival(m, j, 0).wait_recv()
+            for k in range(1, chips):
+                f_arrival(m, j, k).wait_recv()
+            at = slice(j * width, (j + 1) * width)
+            x = gbuf[m, :, :, at].reshape(group * mb, width)
+            part = jnp.dot(x, wq[at, :], preferred_element_type=F32)
+            q = part if q is None else q + part
+            if j + 1 < CHUNKS:
+                pass_on(m, j + 1)
+        q = (q * scaling).astype(BF16)
         block = 0 if blocks == 1 else (m * mb) // BLOCK_LEN
         heads_out = []
         for h in range(heads):
@@ -327,25 +337,25 @@
         begin(0)
 
     wkv_load.wait()
-    spread(1)
-    for k in range(2, chips):
+    for k in range(1, chips):
         spread(k)
-        if k == 2:
-            project(0)
-        share(k - 1)
-    if chips == 2:
-        project(0)
-    share(chips - 1)
     for k in range(1, chips):
-        project(k)
+        share(k)
+        project(k - 1)
+
+    @pl.when(section == 0)
+    def _():
+        pass_on(0)
+
+    project(chips - 1)
 
     @pl.when(section > 0)
     def _():
         begin(0)
+        pass_on(0)
 
     wq_load.wait()
     wo_load.wait()
-    pass_on(0)
 
     def step(m, carry):
         compute(m)
@@ -375,11 +385,11 @@
                 n2_copy(k, j).wait_send()
 
     def drain(m, carry):
-        for k in range(chips):
-            g_copy(m, k).wait_send()
-        for k in range(1, chips):
-            f_copy(m, k).wait_send()
-        for j in range(CHUNKS):
+        for j in range(CHUNKS):
+            for k in range(chips):
+                g_copy(m, j, k).wait_send()
+                if k > 0:
+                    f_copy(m, j, k).wait_send()
             r1_copy(m, j).wait_send()
             for k in range(1, chips):
                 r2_copy(m, j, k).wait_send()
@@ -431,10 +441,10 @@
             dma((chips, sections)),
             dma((micro,)),
             dma((micro,)),
-            dma((micro, chips)),
-            dma((micro, chips)),
-            dma((micro, chips)),
-            dma((micro, chips)),
+            dma((micro, CHUNKS, chips)),
+            dma((micro, CHUNKS, chips)),
+            dma((micro, CHUNKS, chips)),
+            dma((micro, CHUNKS, chips)),
             dma((micro, CHUNKS)),
             dma((micro, CHUNKS)),
             dma((micro, CHUNKS, chips)),

time: 283 us -> 279 us (0.986)
  Pallas kernels: 269 us -> 264 us
    pallas_call x1, Pallas kernels: 269 us -> 264 us  [per_device(): pl.pallas_call(functools.partial(relay_kernel, sections, group), out_shap...]
where the time goes in v3:
time: 279 us; the launch traced here: 275 us
  Pallas kernels  264 us (95%)
  local copies, waits for them, and re-layouts  11.2 us (4%)
    pallas_call x1, Pallas kernels, per_device(): pl.pallas_call(functools.partial(relay_kernel, sections, group), out_shap...  264 us
    unnamed x2, local copies, waits for them, and re-layouts  11.2 us

profile of v3, /device:TPU:7, one launch (start us, length us, event | category | flops | bytes accessed | tf_op | source)
XLA Modules:
  0.0 275.0 jit_solution(2820466176151271450)
XLA Ops:
  0.0 9.3 %copy.7 = bf16[512,8,2,512]{3,1,2,0:T(8,128)(2,1)} copy(bf16[512,8,2,512]{3,2,1,0:T(2,128)(2,1)} %bitcast.9) | data formatting | bytes 16777216
  9.3 263.8 %shard_map.64 = bf16[4,16,4096]{2,1,0:T(8,128)(2,1)} custom-call(bf16[4,16,4096]{2,1,0:T(8,128)(2,1)} %bitcast.14, f32[1,4096]{1,0:T(1,128)} %gain_ref.1, bf16[4096,512]{1,0:T(8,128)(2,1)} %bitcast.10, bf16[4,32,4096]{2,1,0:T(8,128)(2,1)} %bitcast.13, bf16[4096,1024]{1,0:T(8,128)(2,1)} %bitcast.8, bf16[512,4096]{1,0:T(8,128)(2,1)} %bitcast.11), custom_call_target="tpu_custom_call" | custom-call | tf_op jit(solution)/shard_map/pallas_call | solution.py:417
  273.1 1.9 copy.9
